TPU v7x, 32 devices: a whole 2x2x4 slice. The times are simulated.
32 devices in a mesh: section: 2 (over x), head: 4 (over y, core), tok: 4 (over z).
Axes of the slice: x: 2, y: 2, z: 4, core: 2. Of those that a mesh axis runs over, the one named last changes fastest.
Arguments:
- held_cotangents: bfloat16 [2, 2, 512, 2560], P('section', None, 'tok', 'head'), may hold values from -6 to 6
- entering_adjoint: bfloat16 [512, 2560], P('tok', 'head'), may hold values from -6 to 6
- saved_queries: bfloat16 [2, 512, 2560], P('section', 'tok', 'head'), may hold values from -1024 to 1024
- saved_keys: bfloat16 [2, 512, 2560], P('section', 'tok', 'head'), may hold values from -20 to 20
- value_weight: bfloat16 [2, 2560, 2560], P('section', None, 'head'), may hold values from -0.125 to 0.125
- out_weight: bfloat16 [2, 2560, 2560], P('section', 'tok', 'head'), may hold values from -0.125 to 0.125
- block_gate: float32 [2, 2560], P('section'), may hold values from -3 to 3
- time_gate: float32 [32, 2560], replicated, may hold values from -3 to 3
- timestep: int32 [1], replicated, may hold values from 0 to 31
Outputs:
- passed: bfloat16 [2, 2, 512, 2560], P('section', None, 'tok', 'head')
All inputs are finite; a program needn't handle non-finite values.
Results may differ from a plain program's by a relative error of at most 0.0085.
Values may be sent and summed in bfloat16 or wider, within the bound.
No kernel may reach another device: no remote copies, remote signals or barrier semaphores. Data moves between devices by JAX's collectives and lax.ppermute only.
A program may use at most 64 MiB of HBM per device.

v0:
```python
import jax
import jax.numpy as jnp
from jax import lax
from jax.sharding import PartitionSpec as P

HD = 128
GUIDE = 3.0


def combined_all(part, axis, combine):
    gathered = jax.tree.map(lambda a: lax.all_gather(a, axis), part)

    def take(source):
        return jax.tree.map(lambda a: lax.dynamic_index_in_dim(a, source, 0, False), gathered)

    return lax.fori_loop(
        1, lax.axis_size(axis), lambda source, state: combine(state, take(source)), take(0)
    )


def shifted(value, axis, steps):
    count = lax.axis_size(axis)
    leading, last = (max(0, -steps), min(count, count - steps))
    return lax.ppermute(value, axis, [(source, source + steps) for source in range(leading, last)])


def merge_stats(earlier, latter):
    row_top = jnp.maximum(earlier[0], latter[0])
    total_sum = earlier[1] * jnp.exp(earlier[0] - row_top) + latter[1] * jnp.exp(
        latter[0] - row_top
    )
    return (row_top, total_sum)


def body(
    held_cotangents,
    entering_adjoint,
    saved_queries,
    saved_keys,
    value_weight,
    out_weight,
    block_gate,
    time_gate,
    timestep,
):
    steps_index = jnp.arange(time_gate.shape[0])
    time_row = jnp.sum(
        jnp.where((steps_index == timestep[0])[:, None], time_gate, jnp.zeros_like(time_gate)),
        axis=0,
    )
    gate_row = block_gate[0] + time_row
    whole_cot = lax.all_gather(held_cotangents[0], "head", axis=2, tiled=True)
    scaled = (whole_cot.astype(jnp.float32) * gate_row).astype(jnp.bfloat16)
    out_full = lax.all_gather(out_weight[0], "tok", axis=0, tiled=True)
    attn_grad = jnp.einsum(
        "btd,dk->btk", scaled, out_full, preferred_element_type=jnp.float32
    ).astype(jnp.bfloat16)
    rows_here = saved_queries.shape[1]
    groups_here = saved_queries.shape[2] // HD
    score_scale = HD ** (-0.5)
    normal_grad = attn_grad[0]
    query_all = lax.all_gather(saved_queries[0], "tok", axis=0, tiled=True)
    total_rows = query_all.shape[0]
    shards = total_rows // rows_here
    key_heads = saved_keys[0].reshape(rows_here, groups_here, HD)
    scores = (
        jnp.einsum(
            "ihe,jhe->hij",
            query_all.reshape(total_rows, groups_here, HD),
            key_heads,
            preferred_element_type=jnp.float32,
        )
        * score_scale
    )
    row_top = jnp.max(scores, axis=2)
    partial_total = jnp.sum(jnp.exp(scores - row_top[:, :, None]), axis=2)
    top_all, total_all = combined_all((row_top, partial_total), "tok", merge_stats)
    log_total = top_all + jnp.log(total_all)
    weights = jnp.exp(scores - log_total[:, :, None]).astype(jnp.bfloat16)
    grad_all = lax.all_gather(normal_grad, "tok", axis=0, tiled=True)
    blocked = jnp.einsum(
        "hbij,bihe->bjhe",
        weights.reshape(groups_here, shards, rows_here, rows_here),
        grad_all.reshape(shards, rows_here, groups_here, HD),
        preferred_element_type=jnp.float32,
    )
    blocked = lax.optimization_barrier(blocked.astype(jnp.bfloat16))
    value_grad = (
        jnp.sum(blocked.astype(jnp.float32), axis=0)
        .reshape(rows_here, groups_here * HD)
        .astype(jnp.bfloat16)
    )
    stacked = jnp.stack([value_grad, attn_grad[1]])
    partial_back = jnp.einsum(
        "btk,dk->btd", stacked, value_weight[0], preferred_element_type=jnp.float32
    )
    back_sum = lax.psum_scatter(
        partial_back.astype(jnp.bfloat16), "head", scatter_dimension=2, tiled=True
    ).astype(jnp.float32)
    block_cot = (held_cotangents[0].astype(jnp.float32) + back_sum).astype(jnp.bfloat16)
    passed_on = shifted(block_cot, "section", -1)
    entering_full = entering_adjoint.astype(jnp.float32)
    fresh_rows = jnp.stack([(1.0 + GUIDE) * entering_full, -GUIDE * entering_full]).astype(
        jnp.bfloat16
    )
    is_last = lax.axis_index("section") == lax.axis_size("section") - 1
    return jnp.where(is_last, fresh_rows, passed_on)[None]


def solution(mesh):
    return jax.shard_map(
        body,
        mesh=mesh,
        in_specs=(
            P("section", None, "tok", "head"),
            P("tok", "head"),
            P("section", "tok", "head"),
            P("section", "tok", "head"),
            P("section", None, "head"),
            P("section", "tok", "head"),
            P("section", None),
            P(),
            P(),
        ),
        out_specs=P("section", None, "tok", "head"),
        check_vma=False,
    )
```

profile of v0, /device:TPU:0, one launch (start us, length us, event | category | flops | bytes accessed | tf_op | source)
XLA Modules:
  0.0 187.7 jit_solution(18396355772146746361)
XLA Ops:
  6.5 0.7 all-gather.11.cloned.1.call-update
  7.3 0.0 all-gather.13.cloned.1.call-start
  7.3 0.7 all-gather.13.cloned.1.call-update
  8.0 0.0 reduce-scatter.4.cloned.1.call-start
  8.7 1.7 copy.22
  10.4 1.1 copy.23
  11.6 1.1 select_reduce_fusion
  12.7 19.1 %all-gather.3 = bf16[1,512,640]{1,2,0:T(8,128)(2,1)S(1)} all-gather(bf16[1,128,640]{1,2,0:T(8,128)(2,1)} %copy.22), channel_id=5, replica_groups=mesh['section'=2,'head'=4,'tok'=4] {'tok'}, dimensions={1}, use_global_device_ids=true | all-gather | bytes 819200 | tf_op jit(solution)/shard_map/all_gather | solution.py:62
  31.7 0.6 fusion.28
  32.4 13.4 %all-gather.6 = f32[4,5,512]{2,1,0:T(8,128)S(1)} all-gather(f32[1,5,512]{2,1,0:T(8,128)S(1)} %bitcast.70), channel_id=6, replica_groups=mesh['section'=2,'head'=4,'tok'=4] {'tok'}, dimensions={0}, use_global_device_ids=true | all-gather | bytes 51200 | tf_op jit(solution)/shard_map/all_gather | solution.py:11
  45.8 0.8 exponential_reduce_fusion
  46.6 14.1 %all-gather.7 = f32[4,5,512]{2,1,0:T(8,128)S(1)} all-gather(f32[1,5,512]{2,1,0:T(8,128)S(1)} %bitcast.71), channel_id=7, replica_groups=mesh['section'=2,'head'=4,'tok'=4] {'tok'}, dimensions={0}, use_global_device_ids=true | all-gather | bytes 51200 | tf_op jit(solution)/shard_map/all_gather | solution.py:11
  60.7 0.1 while.17
  60.9 2.6 %exponential_convert_fusion = bf16[5,512,128]{2,1,0:T(8,128)(2,1)} fusion(f32[5,512,128]{2,1,0:T(8,128)} %copy-done.1, f32[5,512]{1,0:T(8,128)S(1)} %log_add_fusion), kind=kLoop, calls=%fused_computation.15 | loop fusion | flops 655360 | bytes 1976320 | tf_op jit(solution)/shard_map/convert_element_type | solution.py:79
  63.4 34.6 %all-gather.13.cloned.1.call-done = bf16[1,2560,640]{2,1,0:T(8,128)(2,1)} async-done(((bf16[1,640,640]{2,1,0:T(8,128)(2,1)}), bf16[1,2560,640]{2,1,0:T(8,128)(2,1)}) %all-gather.13.cloned.1.call-update) | async-done | bytes 3276816 | tf_op jit(solution)/shard_map/all_gather | solution.py:54
  98.0 3.5 %fusion.10 = bf16[2,128,640]{2,1,0:T(8,128)(2,1)S(1)} fusion(bf16[1,2560,640]{2,1,0:T(8,128)(2,1)} %all-gather.13.cloned.1.call-done, bf16[1,2,128,2560]{3,2,1,0:T(8,128)(2,1)} %all-gather.11.cloned.1.call-done, f32[2560]{0:T(1024)S(1)} %add.62), kind=kOutput, calls=%fused_computation.19 | convolution fusion | flops 840990720 | bytes 4925440 | tf_op jit(solution)/shard_map/btd,dk->btk/dot_general | solution.py:55
  101.6 0.7 fusion.27
  102.3 17.6 %all-gather.2 = bf16[1,512,640]{2,1,0:T(8,128)(2,1)} all-gather(bf16[1,128,640]{2,1,0:T(8,128)(2,1)S(1)} %get-tuple-element.152), channel_id=4, replica_groups=mesh['section'=2,'head'=4,'tok'=4] {'tok'}, dimensions={1}, use_global_device_ids=true | all-gather | bytes 819200 | tf_op jit(solution)/shard_map/all_gather | solution.py:80
  119.9 2.5 %reshape.61 = bf16[4,128,5,128]{3,2,1,0:T(8,128)(2,1)} reshape(bf16[1,512,640]{2,1,0:T(8,128)(2,1)} %all-gather.2) | data formatting | bytes 1310720 | tf_op jit(solution)/shard_map/reshape | solution.py:84
  122.4 2.7 %fusion.9 = bf16[4,128,5,128]{1,3,2,0:T(8,128)(2,1)} fusion(bf16[4,128,5,128]{3,2,1,0:T(8,128)(2,1)} %reshape.61, bf16[5,4,128,128]{3,2,1,0:T(8,128)(2,1)} %bitcast.66), kind=kOutput, calls=%fused_computation.18 | convolution fusion | flops 84213760 | bytes 1966080 | tf_op jit(solution)/shard_map/hbij,bihe->bjhe/dot_general | solution.py:81
  125.1 1.2 reduce_sum.32
  126.3 0.8 copy.28
  127.1 3.3 %convolution_convert_fusion = bf16[2,128,2560]{2,1,0:T(8,128)(2,1)} fusion(bf16[1,2560,640]{2,1,0:T(8,128)(2,1)S(1)} %copy-done, bf16[1,128,640]{2,1,0:T(8,128)(2,1)} %get-tuple-element.153, bf16[1,128,640]{2,1,0:T(8,128)(2,1)} %copy.28), kind=kOutput, calls=%fused_computation.5 | convolution fusion | flops 839680000 | bytes 4915200 | tf_op jit(solution)/shard_map/btk,dk->btd/dot_general | solution.py:94
  130.4 4.3 %copy.33 = bf16[2,128,2560]{1,0,2:T(2,128)(2,1)} copy(bf16[2,128,2560]{2,1,0:T(8,128)(2,1)} %convolution_convert_fusion) | data formatting | bytes 2621440
  134.7 2.6 %copy.41 = bf16[320,8,2,128]{3,1,2,0:T(8,128)(2,1)} copy(bf16[320,8,2,128]{3,2,1,0:T(2,128)(2,1)} %bitcast.64) | data formatting | bytes 2621440
  137.3 25.1 %reduce-scatter.4.cloned.1.call-done = bf16[640,256]{1,0:T(8,128)(2,1)} async-done(((bf16[2560,256]{1,0:T(8,128)(2,1)}), bf16[640,256]{1,0:T(8,128)(2,1)}) %reduce-scatter.4.cloned.1.call-update) | async-done | bytes 327696
  162.4 1.8 reshape.63
  164.1 1.9 %copy.34 = bf16[2,128,640]{2,1,0:T(8,128)(2,1)} copy(bf16[2,128,640]{1,0,2:T(2,128)(2,1)} %bitcast.67) | data formatting | bytes 655360
  166.1 1.9 fusion.15
  167.9 1.3 collective-permute-start
  169.3 10.1 %collective-permute-done = bf16[2,128,640]{2,1,0:T(8,128)(2,1)} collective-permute-done((bf16[2,128,640]{2,1,0:T(8,128)(2,1)}, bf16[2,128,640]{2,1,0:T(8,128)(2,1)}, u32[]{:S(2)}, u32[]{:S(2)}) %collective-permute-start) | collective-permute-done | bytes 327712 | tf_op jit(solution)/shard_map/ppermute | solution.py:24
  179.4 1.7 fusion.20
  (21 shorter events, 0.2 us)
Async XLA Ops:
  6.5 120.6 %copy-start = (bf16[1,2560,640]{2,1,0:T(8,128)(2,1)S(1)}, bf16[1,2560,640]{2,1,0:T(8,128)(2,1)}, u32[]{:S(2)}) copy-start(bf16[1,2560,640]{2,1,0:T(8,128)(2,1)} %param.15) | copy-start | bytes 9830404
  6.5 5.0 %copy-start.3 = (f32[1,2560]{1,0:T(1,128)S(1)}, f32[1,2560]{1,0:T(1,128)}, u32[]{:S(2)}) copy-start(f32[1,2560]{1,0:T(1,128)} %param.17) | copy-start | bytes 30724
  6.5 56.9 %all-gather.11.cloned.1.call-start = ((), (), s32[]{:S(2)}) async-start(), calls=%async_computation.1 | async-start | bytes 1638400 | tf_op jit(solution)/shard_map/all_gather | solution.py:52
  7.3 90.8 %all-gather.13.cloned.1.call-start = ((), (), s32[]{:S(2)}) async-start(), calls=%async_computation.2 | async-start | bytes 4096000 | tf_op jit(solution)/shard_map/all_gather | solution.py:54
  8.0 154.4 %reduce-scatter.4.cloned.1.call-start = ((), (), s32[]{:S(2)}) async-start(), calls=%async_computation.3 | async-start | bytes 1638400
  32.4 13.4 %copy-start.1 = (f32[5,512,128]{2,1,0:T(8,128)}, f32[5,512,128]{2,1,0:T(8,128)S(1)}, u32[]{:S(2)}) copy-start(f32[5,512,128]{2,1,0:T(8,128)S(1)} %get-tuple-element.157) | copy-start | bytes 3932164
  137.3 32.0 %copy-start.2 = (bf16[128,640]{1,0:T(8,128)(2,1)S(1)}, bf16[128,640]{1,0:T(8,128)(2,1)}, u32[]{:S(2)}) copy-start(bf16[128,640]{1,0:T(8,128)(2,1)} %param.12) | copy-start | bytes 491524
  167.9 11.5 %collective-permute-start = (bf16[2,128,640]{2,1,0:T(8,128)(2,1)}, bf16[2,128,640]{2,1,0:T(8,128)(2,1)}, u32[]{:S(2)}, u32[]{:S(2)}) collective-permute-start(bf16[2,128,640]{2,1,0:T(8,128)(2,1)} %fusion.15), channel_id=1, source_target_pairs={{16,0},{17,1},{18,2},{19,3},{20,4},{21,5},{22,6},{23,7},{24,8},{25... | collective-permute-start | bytes 983048 | tf_op jit(solution)/shard_map/ppermute | solution.py:24
Sparse Core Ops, SparseCore 0:
  8.9 20.8 all-gather.10
  31.4 66.6 all-gather.12
  137.4 24.9 reduce-scatter.3
where the time goes:
time: 188 us
  waiting for transfers between devices  71.2 us (38%)
  blocking collectives  64.3 us (34%)
  local copies, waits for them, and re-layouts  17.4 us (9%)
  between operations  13.9 us (7%)
  matrix products  10.1 us (5%)
  other arithmetic  9.44 us (5%)
    all_gather x1, waiting for transfers between devices, body(): out_full = lax.all_gather(out_weight[0], 'tok', axis=0, tiled=True)  34.6 us
    all_gather x2, blocking collectives, combined_all(): gathered = jax.tree.map(lambda a: lax.all_gather(a, axis), part)  27.5 us
    unnamed x4, waiting for transfers between devices  26.5 us
    all_gather x1, blocking collectives, body(): query_all = lax.all_gather(saved_queries[0], 'tok', axis=0, tiled=True)  19.1 us
    all_gather x1, blocking collectives, body(): grad_all = lax.all_gather(normal_grad, 'tok', axis=0, tiled=True)  17.6 us
    unnamed x14, local copies, waits for them, and re-layouts  13.3 us
    ppermute x1, waiting for transfers between devices, shifted(): lax.ppermute(value, axis, [(source, source + steps) for source in range(l...  10.1 us
  transfers between devices with their start and end apart: 4, of which 3 were waited for; matrix products, arithmetic and copies ran while one was open for 4% of the time, Pallas kernels for 0%

commit v1 on v0

--- a/solution.py
+++ b/solution.py
@@ -77,7 +77,12 @@
     top_all, total_all = combined_all((row_top, partial_total), "tok", merge_stats)
     log_total = top_all + jnp.log(total_all)
     weights = jnp.exp(scores - log_total[:, :, None]).astype(jnp.bfloat16)
-    grad_all = lax.all_gather(normal_grad, "tok", axis=0, tiled=True)
+    ring = [normal_grad]
+    for hop in range(3):
+        ring.append(lax.ppermute(ring[-1], "tok", [(dev, (dev + 1) % 4) for dev in range(4)]))
+    grad_all = jnp.roll(
+        jnp.concatenate(ring[::-1], axis=0), (lax.axis_index("tok") + 1) * ring[0].shape[0], axis=0
+    )
     blocked = jnp.einsum(
         "hbij,bihe->bjhe",
         weights.reshape(groups_here, shards, rows_here, rows_here),

time: 188 us -> 195 us (1.037)
  waiting for transfers between devices: 71.2 us -> 90.8 us
  blocking collectives: 64.3 us -> 46.6 us
  other arithmetic: 9.44 us -> 11.6 us
    all_gather x1 -> x0, blocking collectives: 17.6 us -> none  [body(): grad_all = lax.all_gather(normal_grad, 'tok', axis=0, tiled=True)]
    ppermute x0 -> x3, waiting for transfers between devices: none -> 17.1 us  [body(): lax.ppermute(ring[-1], 'tok', [(dev, (dev + 1) % 4) for dev in range(4)])]
    all_gather x1, waiting for transfers between devices: 34.6 us -> 37.3 us  [body(): out_full = lax.all_gather(out_weight[0], 'tok', axis=0, tiled=True)]
    add x3, other arithmetic: 0.06 us -> 2.22 us  [merge_stats(): earlier[1] * jnp.exp(earlier[0] - row_top)]
    unnamed x14 -> x27, local copies, waits for them, and re-layouts: 13.3 us -> 14.2 us
  transfers between devices with their start and end apart: 4 -> 7, of which waited for: 3 -> 6; matrix products, arithmetic and copies ran while one was open for 4% -> 5% of each run, Pallas kernels for 0% -> 0%
where the time goes in v1:
time: 195 us; the launch traced here: 194 us
  waiting for transfers between devices  90.8 us (47%)
  blocking collectives  46.6 us (24%)
  local copies, waits for them, and re-layouts  19.3 us (10%)
  between operations  14 us (7%)
  other arithmetic  11.6 us (6%)
  matrix products  10.1 us (5%)
    all_gather x1, waiting for transfers between devices, body(): out_full = lax.all_gather(out_weight[0], 'tok', axis=0, tiled=True)  37.3 us
    all_gather x2, blocking collectives, combined_all(): gathered = jax.tree.map(lambda a: lax.all_gather(a, axis), part)  27.5 us
    unnamed x4, waiting for transfers between devices  26.2 us
    all_gather x1, blocking collectives, body(): query_all = lax.all_gather(saved_queries[0], 'tok', axis=0, tiled=True)  19.1 us
    ppermute x3, waiting for transfers between devices, body(): lax.ppermute(ring[-1], 'tok', [(dev, (dev + 1) % 4) for dev in range(4)])  17.1 us
    unnamed x27, local copies, waits for them, and re-layouts  14.2 us
    ppermute x1, waiting for transfers between devices, shifted(): lax.ppermute(value, axis, [(source, source + steps) for source in range(l...  10.1 us
  transfers between devices with their start and end apart: 7, of which 6 were waited for; matrix products, arithmetic and copies ran while one was open for 5% of the time, Pallas kernels for 0%

profile of v1, /device:TPU:0, one launch (start us, length us, event | category | flops | bytes accessed | tf_op | source)
XLA Modules:
  0.0 193.8 jit_solution(16527352367496950164)
XLA Ops:
  8.7 1.7 copy.21
  10.4 1.1 copy.22
  11.6 1.1 select_reduce_fusion
  12.7 19.1 %all-gather.2 = bf16[1,512,640]{1,2,0:T(8,128)(2,1)S(1)} all-gather(bf16[1,128,640]{1,2,0:T(8,128)(2,1)} %copy.21), channel_id=4, replica_groups=mesh['section'=2,'head'=4,'tok'=4] {'tok'}, dimensions={1}, use_global_device_ids=true | all-gather | bytes 819200 | tf_op jit(solution)/shard_map/all_gather | solution.py:62
  32.4 13.4 %all-gather.5 = f32[4,5,512]{2,1,0:T(8,128)S(1)} all-gather(f32[1,5,512]{2,1,0:T(8,128)S(1)} %bitcast.76), channel_id=5, replica_groups=mesh['section'=2,'head'=4,'tok'=4] {'tok'}, dimensions={0}, use_global_device_ids=true | all-gather | bytes 51200 | tf_op jit(solution)/shard_map/all_gather | solution.py:11
  45.8 0.8 exponential_reduce_fusion
  46.6 14.1 %all-gather.6 = f32[4,5,512]{2,1,0:T(8,128)S(1)} all-gather(f32[1,5,512]{2,1,0:T(8,128)S(1)} %bitcast.77), channel_id=6, replica_groups=mesh['section'=2,'head'=4,'tok'=4] {'tok'}, dimensions={0}, use_global_device_ids=true | all-gather | bytes 51200 | tf_op jit(solution)/shard_map/all_gather | solution.py:11
  60.7 37.3 %all-gather.12.cloned.1.call-done = bf16[1,2560,640]{2,1,0:T(8,128)(2,1)} async-done(((bf16[1,640,640]{2,1,0:T(8,128)(2,1)}), bf16[1,2560,640]{2,1,0:T(8,128)(2,1)}) %all-gather.12.cloned.1.call-update) | async-done | bytes 3276816 | tf_op jit(solution)/shard_map/all_gather | solution.py:54
  98.0 3.5 %fusion.10 = bf16[2,128,640]{2,1,0:T(8,128)(2,1)S(1)} fusion(bf16[1,2560,640]{2,1,0:T(8,128)(2,1)} %all-gather.12.cloned.1.call-done, bf16[1,2,128,2560]{3,2,1,0:T(8,128)(2,1)} %all-gather.10.cloned.1.call-done, f32[2560]{0:T(1024)S(1)} %add.75), kind=kOutput, calls=%fused_computation.19 | convolution fusion | flops 840990720 | bytes 4925440 | tf_op jit(solution)/shard_map/btd,dk->btk/dot_general | solution.py:55
  102.3 0.8 slice_bitcast_fusion
  103.1 2.3 %while.17 = (s32[]{:T(128)}, f32[5,512]{1,0:T(8,128)S(1)}, f32[5,512]{1,0:T(8,128)S(1)}, f32[4,5,512]{2,1,0:T(8,128)S(1)}, f32[4,5,512]{2,1,0:T(8,128)}, /*index=5*/s32[]{:T(128)}, s32[]{:T(128)}, s32[]{:T(128)}) while((s32[]{:T(128)}, f32[5,512]{1,0:T(8,128)S(1)}, f32[5,512]{1,0:T(8,128)S(1)}, f32[4,5,512]{2,1,0:T(8,128)S(1)}, ...), condition=%wide.region_4.5_spmd, body=%wide.region_3.4_spmd.sunk | while | flops 15365 | bytes 61571 | solution.py:16
  103.8 0.7 fusion.31
  104.6 0.7 fusion.31
  105.4 5.6 %collective-permute-done = bf16[128,640]{1,0:T(8,128)(2,1)S(1)} collective-permute-done((bf16[128,640]{1,0:T(8,128)(2,1)}, bf16[128,640]{1,0:T(8,128)(2,1)S(1)}, u32[]{:S(2)}, u32[]{:S(2)}) %collective-permute-start) | collective-permute-done | bytes 163872 | tf_op jit(solution)/shard_map/ppermute | solution.py:82
  110.9 7.1 %collective-permute-done.1 = bf16[128,640]{1,0:T(8,128)(2,1)S(1)} collective-permute-done((bf16[128,640]{1,0:T(8,128)(2,1)S(1)}, bf16[128,640]{1,0:T(8,128)(2,1)S(1)}, u32[]{:S(2)}, u32[]{:S(2)}) %collective-permute-start.1) | collective-permute-done | bytes 163872 | tf_op jit(solution)/shard_map/ppermute | solution.py:82
  118.0 2.6 %exponential_convert_fusion = bf16[5,512,128]{2,1,0:T(8,128)(2,1)} fusion(f32[5,512,128]{2,1,0:T(8,128)} %copy-done.1, f32[5,512]{1,0:T(8,128)S(1)} %log_add_fusion), kind=kLoop, calls=%fused_computation.15 | loop fusion | flops 655360 | bytes 1976320 | tf_op jit(solution)/shard_map/convert_element_type | solution.py:79
  120.7 4.5 %collective-permute-done.2 = bf16[128,640]{1,0:T(8,128)(2,1)S(1)} collective-permute-done((bf16[128,640]{1,0:T(8,128)(2,1)S(1)}, bf16[128,640]{1,0:T(8,128)(2,1)S(1)}, u32[]{:S(2)}, u32[]{:S(2)}) %collective-permute-start.2) | collective-permute-done | bytes 163872 | tf_op jit(solution)/shard_map/ppermute | solution.py:82
  125.4 0.9 constant_dynamic-slice_fusion
  126.3 2.5 %reshape.59 = bf16[4,128,5,128]{3,2,1,0:T(8,128)(2,1)} reshape(bf16[512,640]{1,0:T(8,128)(2,1)} %constant_dynamic-slice_fusion) | data formatting | bytes 1310720 | tf_op jit(solution)/shard_map/reshape | solution.py:89
  128.8 2.6 %fusion.9 = bf16[4,128,5,128]{1,3,2,0:T(8,128)(2,1)} fusion(bf16[4,128,5,128]{3,2,1,0:T(8,128)(2,1)} %reshape.59, bf16[5,4,128,128]{3,2,1,0:T(8,128)(2,1)} %bitcast.72), kind=kOutput, calls=%fused_computation.18 | convolution fusion | flops 84213760 | bytes 1966080 | tf_op jit(solution)/shard_map/hbij,bihe->bjhe/dot_general | solution.py:86
  131.5 1.2 reduce_sum.32
  132.7 0.8 copy.27
  133.5 3.3 %convolution_convert_fusion = bf16[2,128,2560]{2,1,0:T(8,128)(2,1)} fusion(bf16[1,2560,640]{2,1,0:T(8,128)(2,1)S(1)} %copy-done, bf16[1,128,640]{2,1,0:T(8,128)(2,1)} %get-tuple-element.153, bf16[1,128,640]{2,1,0:T(8,128)(2,1)} %copy.27), kind=kOutput, calls=%fused_computation.5 | convolution fusion | flops 839680000 | bytes 4915200 | tf_op jit(solution)/shard_map/btk,dk->btd/dot_general | solution.py:99
  136.8 4.3 %copy.32 = bf16[2,128,2560]{1,0,2:T(2,128)(2,1)} copy(bf16[2,128,2560]{2,1,0:T(8,128)(2,1)} %convolution_convert_fusion) | data formatting | bytes 2621440
  141.1 2.6 %copy.40 = bf16[320,8,2,128]{3,1,2,0:T(8,128)(2,1)} copy(bf16[320,8,2,128]{3,2,1,0:T(2,128)(2,1)} %bitcast.70) | data formatting | bytes 2621440
  143.7 24.8 %reduce-scatter.4.cloned.1.call-done = bf16[640,256]{1,0:T(8,128)(2,1)} async-done(((bf16[2560,256]{1,0:T(8,128)(2,1)}), bf16[640,256]{1,0:T(8,128)(2,1)}) %reduce-scatter.4.cloned.1.call-update) | async-done | bytes 327696
  168.4 1.8 reshape.61
  170.2 1.9 copy.33
  172.1 1.9 fusion.15
  174.0 1.3 collective-permute-start.3
  175.4 10.1 %collective-permute-done.3 = bf16[2,128,640]{2,1,0:T(8,128)(2,1)} collective-permute-done((bf16[2,128,640]{2,1,0:T(8,128)(2,1)}, bf16[2,128,640]{2,1,0:T(8,128)(2,1)}, u32[]{:S(2)}, u32[]{:S(2)}) %collective-permute-start.3) | collective-permute-done | bytes 327712 | tf_op jit(solution)/shard_map/ppermute | solution.py:24
  185.5 1.7 fusion.20
  (41 shorter events, 3.9 us)
Async XLA Ops:
  6.5 127.0 %copy-start = (bf16[1,2560,640]{2,1,0:T(8,128)(2,1)S(1)}, bf16[1,2560,640]{2,1,0:T(8,128)(2,1)}, u32[]{:S(2)}) copy-start(bf16[1,2560,640]{2,1,0:T(8,128)(2,1)} %param.15) | copy-start | bytes 9830404
  6.5 5.0 %copy-start.6 = (f32[1,2560]{1,0:T(1,128)S(1)}, f32[1,2560]{1,0:T(1,128)}, u32[]{:S(2)}) copy-start(f32[1,2560]{1,0:T(1,128)} %param.17) | copy-start | bytes 30724
  6.5 54.2 %all-gather.10.cloned.1.call-start = ((), (), s32[]{:S(2)}) async-start(), calls=%async_computation.1 | async-start | bytes 1638400 | tf_op jit(solution)/shard_map/all_gather | solution.py:52
  7.3 90.8 %all-gather.12.cloned.1.call-start = ((), (), s32[]{:S(2)}) async-start(), calls=%async_computation.2 | async-start | bytes 4096000 | tf_op jit(solution)/shard_map/all_gather | solution.py:54
  8.0 160.4 %reduce-scatter.4.cloned.1.call-start = ((), (), s32[]{:S(2)}) async-start(), calls=%async_computation.3 | async-start | bytes 1638400
  32.4 13.4 %copy-start.1 = (f32[5,512,128]{2,1,0:T(8,128)}, f32[5,512,128]{2,1,0:T(8,128)S(1)}, u32[]{:S(2)}) copy-start(f32[5,512,128]{2,1,0:T(8,128)S(1)} %get-tuple-element.157) | copy-start | bytes 3932164
  60.7 40.9 %copy-start.4 = (f32[4,5,512]{2,1,0:T(8,128)}, f32[4,5,512]{2,1,0:T(8,128)S(1)}, u32[]{:S(2)}) copy-start(f32[4,5,512]{2,1,0:T(8,128)S(1)} %all-gather.6) | copy-start | bytes 122884
  101.6 0.7 copy-start.2
  103.1 7.8 %collective-permute-start = (bf16[128,640]{1,0:T(8,128)(2,1)}, bf16[128,640]{1,0:T(8,128)(2,1)S(1)}, u32[]{:S(2)}, u32[]{:S(2)}) collective-permute-start(bf16[128,640]{1,0:T(8,128)(2,1)} %get-tuple-element.152), channel_id=1, source_target_pairs={{0,1},{1,2},{2,3},{3,0},{4,5},{5,6},{6,7},{7,4},{8,9},{9,10},{10,1... | collective-permute-start | bytes 491528 | tf_op jit(solution)/shard_map/ppermute | solution.py:82
  110.9 7.1 %collective-permute-start.1 = (bf16[128,640]{1,0:T(8,128)(2,1)S(1)}, bf16[128,640]{1,0:T(8,128)(2,1)S(1)}, u32[]{:S(2)}, u32[]{:S(2)}) collective-permute-start(bf16[128,640]{1,0:T(8,128)(2,1)S(1)} %collective-permute-done), channel_id=1, source_target_pairs={{0,1},{1,2},{2,3},{3,0},{4,5},{5,6},{6,7},{7,4},{8,9},{9,10},{10,1... | collective-permute-start | bytes 491528 | tf_op jit(solution)/shard_map/ppermute | solution.py:82
  110.9 14.3 %copy-start.3 = (bf16[2,128,640]{2,1,0:T(8,128)(2,1)S(1)}, bf16[2,128,640]{2,1,0:T(8,128)(2,1)}, u32[]{:S(2)}) copy-start(bf16[2,128,640]{2,1,0:T(8,128)(2,1)} %copy-done.2) | copy-start | bytes 983044
  118.0 7.1 %collective-permute-start.2 = (bf16[128,640]{1,0:T(8,128)(2,1)S(1)}, bf16[128,640]{1,0:T(8,128)(2,1)S(1)}, u32[]{:S(2)}, u32[]{:S(2)}) collective-permute-start(bf16[128,640]{1,0:T(8,128)(2,1)S(1)} %collective-permute-done.1), channel_id=1, source_target_pairs={{0,1},{1,2},{2,3},{3,0},{4,5},{5,6},{6,7},{7,4},{8,9},{9,10},{10,1... | collective-permute-start | bytes 491528 | tf_op jit(solution)/shard_map/ppermute | solution.py:82
  143.7 31.6 %copy-start.5 = (bf16[128,640]{1,0:T(8,128)(2,1)S(1)}, bf16[128,640]{1,0:T(8,128)(2,1)}, u32[]{:S(2)}) copy-start(bf16[128,640]{1,0:T(8,128)(2,1)} %param.12) | copy-start | bytes 491524
  174.0 11.5 %collective-permute-start.3 = (bf16[2,128,640]{2,1,0:T(8,128)(2,1)}, bf16[2,128,640]{2,1,0:T(8,128)(2,1)}, u32[]{:S(2)}, u32[]{:S(2)}) collective-permute-start(bf16[2,128,640]{2,1,0:T(8,128)(2,1)} %fusion.15), channel_id=1, source_target_pairs={{16,0},{17,1},{18,2},{19,3},{20,4},{21,5},{22,6},{23,7},{24,8},{25... | collective-permute-start | bytes 983048 | tf_op jit(solution)/shard_map/ppermute | solution.py:24
Sparse Core Ops, SparseCore 0:
  8.9 20.8 all-gather.9
  31.4 66.6 all-gather.11
  143.8 24.6 reduce-scatter.3
